TPU v7x, 32 devices: a whole 2x2x4 slice. The times are simulated.
32 devices in a mesh: body: 16 (over z, x, core), row: 2 (over y).
Axes of the slice: x: 2, y: 2, z: 4, core: 2. Of those that a mesh axis runs over, the one named last changes fastest.
Arguments:
- strengths: bfloat16 [32, 131072], P(None, ('body', 'row')), may hold values from -6 to 6
- influence: bfloat16 [16, 2, 5, 32, 2, 128, 128], P('body', 'row'), may hold values from -0.09375 to 0.09375
- target_block: int32 [16, 2, 5, 32], P('body', 'row'), may hold values from 0 to 31
- source_block: int32 [16, 2, 5, 32], P('body', 'row'), may hold values from 0 to 63
- live_counts: int32 [16, 2, 5], P('body', 'row'), may hold values from 4 to 32, as said below
Outputs:
- response: float32 [32, 131072], P(None, ('body', 'row'))
Inputs may be any that keep to these rules, and one draw needn't show every extreme that they name: Slot k of a slice for source offset t is live when k < live_counts; for offset 2 (the group's own bodies) all 32 slots are live.
All inputs are finite; a program needn't handle non-finite values.
Results may differ from a plain program's by a relative error of at most 0.0003.
Values may be sent and summed in bfloat16 or wider, within the bound.
No kernel may reach another device: no remote copies, remote signals or barrier semaphores. Data moves between devices by JAX's collectives and lax.ppermute only.
A program may use at most 64 MiB of HBM per device.

v0:
```python
import jax
import jax.numpy as jnp
from jax import lax
from jax.sharding import PartitionSpec as P


def passed_along(array, axis, by):
    devices = lax.axis_size(axis)
    return lax.ppermute(array, axis, [(i, (i + by) % devices) for i in range(devices)])


def block_terms(slot_tiles, slot_rows, live_count, picked, row_blocks):
    channels = picked.shape[0]
    heads = channels // 2
    capacity = slot_tiles.shape[0]
    products = jnp.einsum("kprj,hkj->kphr", slot_tiles, picked, preferred_element_type=jnp.float32)
    real_part = products[:, 0, :heads] - products[:, 1, heads:]
    imag_part = products[:, 0, heads:] + products[:, 1, :heads]
    combined = jnp.concatenate([real_part, imag_part], axis=1)
    alive_mask = (jnp.arange(capacity, dtype=jnp.int32) < live_count).astype(jnp.float32)
    onehot = (slot_rows[:, None] == jnp.arange(row_blocks, dtype=jnp.int32)[None, :]).astype(
        jnp.float32
    )
    onehot = onehot * alive_mask[:, None]
    return jnp.einsum("kn,khr->hnr", onehot, combined, precision=lax.Precision.HIGHEST)


def pick_blocks(group_x, slot_cols, block_size):
    channels = group_x.shape[0]
    blocks = group_x.reshape(channels, -1, block_size)
    return jnp.take(blocks, slot_cols, axis=1)


def window(values, reach):
    windows = [(0, values)]
    for direction in (1, -1):
        current = values
        for hop_index in range(reach):
            current = passed_along(current, "body", direction)
            windows.append((-direction * (hop_index + 1), current))
    return windows


def on_device(strengths, influence, target_block, source_block, live_counts):
    channels, row_count = strengths.shape
    block_size = influence.shape[-1]
    row_blocks = row_count // block_size
    reach = (influence.shape[2] - 1) // 2
    totals = (0.5 * strengths.astype(jnp.float32)).reshape(channels, row_blocks, block_size)

    def apply_picked(totals_now, offset, picked):
        index = offset + reach
        return totals_now + block_terms(
            influence[0, 0, index],
            target_block[0, 0, index],
            live_counts[0, 0, index],
            picked,
            row_blocks,
        )

    def apply_offset(totals_now, offset, group_x):
        index = offset + reach
        picked = pick_blocks(group_x, source_block[0, 0, index], block_size)
        return apply_picked(totals_now, offset, picked)

    group_x = lax.all_gather(strengths, "row", axis=1, tiled=True)
    for offset, source_x in window(group_x, reach):
        totals = apply_offset(totals, offset, source_x)
    return totals.reshape(channels, row_count)


def solution(mesh):
    return jax.shard_map(
        on_device,
        mesh=mesh,
        in_specs=(
            P(None, ("body", "row")),
            P("body", "row", None, None, None, None, None),
            P("body", "row", None, None),
            P("body", "row", None, None),
            P("body", "row", None),
        ),
        out_specs=P(None, ("body", "row")),
        check_vma=False,
    )
```

profile of v0, /device:TPU:1, one launch (start us, length us, event | category | flops | bytes accessed | tf_op | source)
XLA Modules:
  0.0 56.6 jit_solution(6832906776811036869)
XLA Ops:
  0.0 9.0 %all_gather.3 = bf16[32,8192]{1,0:T(8,128)(2,1)S(1)} all-gather(bf16[32,4096]{1,0:T(8,128)(2,1)} %param.7), channel_id=1, replica_groups=mesh['body'=16,'row'=2] {'row'}, dimensions={1}, use_global_device_ids=true | all-gather | bytes 786432 | tf_op jit(solution)/shard_map/all_gather | solution.py:66
  9.0 2.5 %collective-permute-start = (bf16[32,8192]{1,0:T(8,128)(2,1)S(1)}, bf16[32,8192]{1,0:T(8,128)(2,1)S(1)}, u32[]{:S(2)}, u32[]{:S(2)}) collective-permute-start(bf16[32,8192]{1,0:T(8,128)(2,1)S(1)} %all_gather.3), channel_id=1, source_target_pairs={{0,2},{2,4},{4,6},{6,8},{8,10},{10,12},{12,14},{14,16},{16,18},{18... | collective-permute-start | bytes 1572872 | tf_op jit(solution)/shard_map/ppermute | solution.py:9
  11.6 1.0 %multiply_bitcast_fusion = f32[4,8,32,128]{3,1,2,0:T(8,128)S(1)} fusion(bf16[32,4096]{1,0:T(8,128)(2,1)} %param.7), kind=kLoop, calls=%fused_computation.51 | loop fusion | flops 262144 | bytes 786432
  12.6 0.7 %compare_and_fusion = (pred[32]{0:T(512)(128)(4,1)S(1)}, s32[32]{0:T(128)S(1)}, pred[32]{0:T(512)(128)(4,1)S(1)}, s32[32]{0:T(128)S(1)}, pred[32]{0:T(512)(128)(...) fusion(s32[1,1,5,32]{3,1,2,0:T(1,128)} %param.10), kind=kLoop, calls=%fused_computation.142 | loop fusion | flops 960 | bytes 1440 | tf_op jit(solution)/shard_map/jit(_take)/and | solution.py:31
  13.4 1.5 %fusion.110 = (s32[1,1,1]{2,1,0:T(1,128)}, s32[1,1,1]{2,1,0:T(1,128)}, s32[1,1,1]{2,1,0:T(1,128)}, s32[1,1,1]{2,1,0:T(1,128)}, s32[1,1,1]{2,1,0:T(1,128)}) fusion(s32[1,1,5]{2,1,0:T(1,128)} %param.11), kind=kLoop, calls=%fused_computation.167 | loop fusion | bytes 40 | tf_op jit(solution)/shard_map/slice | solution.py:56
  16.1 0.6 %compare_convert_fusion.1 = f32[32]{0:T(128)S(1)} fusion(s32[]{:T(128)} %bitcast.45), kind=kLoop, calls=%fused_computation.148 | loop fusion | flops 64 | bytes 132 | tf_op jit(solution)/shard_map/convert_element_type | solution.py:20
  17.3 2.4 %fusion.15 = f32[32,2,32,128]{3,2,1,0:T(8,128)S(1)} fusion(bf16[1,1,5,32,2,128,128]{6,5,4,3,2,1,0:T(8,128)(2,1)} %param.8, bf16[32,32,128]{2,1,0:T(8,128)(2,1)S(1)} %gather_fusion, pred[32]{0:T(512)(128)(4,1)S(1)} %get-tuple-element.25), kind=kOutput, calls=%fused_computation.20 | convolution fusion | flops 67239936 | bytes 3407904 | tf_op jit(solution)/shard_map/kprj,hkj->kphr/dot_general | solution.py:16
  20.6 0.7 %compare_convert_fusion = f32[32]{0:T(128)S(1)} fusion(s32[]{:T(128)} %bitcast.57), kind=kLoop, calls=%fused_computation.147 | loop fusion | flops 64 | bytes 132 | tf_op jit(solution)/shard_map/convert_element_type | solution.py:20
  21.3 0.7 %slice_bitcast_fusion.10 = (s32[32]{0:T(128)S(1)}, s32[32]{0:T(128)S(1)}, s32[32]{0:T(128)S(1)}, s32[32]{0:T(128)S(1)}, s32[32]{0:T(128)S(1)}) fusion(s32[1,1,5,32]{3,1,2,0:T(1,128)} %param.9), kind=kLoop, calls=%fused_computation.152 | loop fusion | bytes 1280 | tf_op jit(solution)/shard_map/eq | solution.py:21
  22.1 1.2 %collective-permute-done = bf16[32,8192]{1,0:T(8,128)(2,1)S(1)} collective-permute-done((bf16[32,8192]{1,0:T(8,128)(2,1)S(1)}, bf16[32,8192]{1,0:T(8,128)(2,1)S(1)}, u32[]{:S(2)}, u32[]{:S(2)}) %collective-permute-start) | collective-permute-done | bytes 524320 | tf_op jit(solution)/shard_map/ppermute | solution.py:9
  24.0 2.4 %fusion.18 = f32[32,2,32,128]{3,2,1,0:T(8,128)S(1)} fusion(bf16[1,1,5,32,2,128,128]{6,5,4,3,2,1,0:T(8,128)(2,1)} %param.8, bf16[32,32,128]{2,1,0:T(8,128)(2,1)S(1)} %gather_fusion.1, pred[32]{0:T(512)(128)(4,1)S(1)} %get-tuple-element.23), kind=kOutput, calls=%fused_computation.21 | convolution fusion | flops 67239936 | bytes 3407904 | tf_op jit(solution)/shard_map/kprj,hkj->kphr/dot_general | solution.py:16
  26.5 1.1 %copy_bitcast_fusion.2 = bf16[32,64,128]{2,0,1:T(8,128)(2,1)S(1)} fusion(bf16[32,8192]{1,0:T(8,128)(2,1)} %collective-permute-done.2), kind=kLoop, calls=%fused_computation.37 | loop fusion | bytes 1048576 | tf_op jit(solution)/shard_map/reshape | solution.py:30
  28.2 2.4 %fusion.24 = f32[32,2,32,128]{3,2,1,0:T(8,128)S(1)} fusion(bf16[1,1,5,32,2,128,128]{6,5,4,3,2,1,0:T(8,128)(2,1)} %param.8, bf16[32,32,128]{2,1,0:T(8,128)(2,1)S(1)} %gather_fusion.3, pred[32]{0:T(512)(128)(4,1)S(1)} %get-tuple-element.27), kind=kOutput, calls=%fused_computation.23 | convolution fusion | flops 67239936 | bytes 3407904 | tf_op jit(solution)/shard_map/kprj,hkj->kphr/dot_general | solution.py:16
  30.8 2.5 %collective-permute-start.1 = (bf16[32,8192]{1,0:T(8,128)(2,1)S(1)}, bf16[32,8192]{1,0:T(8,128)(2,1)S(1)}, u32[]{:S(2)}, u32[]{:S(2)}) collective-permute-start(bf16[32,8192]{1,0:T(8,128)(2,1)S(1)} %collective-permute-done), channel_id=1, source_target_pairs={{0,2},{2,4},{4,6},{6,8},{8,10},{10,12},{12,14},{14,16},{16,18},{18... | collective-permute-start | bytes 1572872 | tf_op jit(solution)/shard_map/ppermute | solution.py:9
  33.5 0.9 %convolution_bitcast_fusion.3 = f32[32,32,128]{2,1,0:T(8,128)S(1)} fusion(f32[32,32,128]{2,1,0:T(8,128)S(1)} %pad_maximum_fusion.1, f32[32]{0:T(128)S(1)} %compare_convert_fusion.3, s32[32]{0:T(128)S(1)} %get-tuple-element.18), kind=kOutput, calls=%fused_computation.28 | convolution fusion | flops 50333696 | bytes 1048832 | tf_op jit(solution)/shard_map/kn,khr->hnr/dot_general | solution.py:25
  34.4 0.9 %convolution_bitcast_fusion.1 = f32[32,32,128]{2,1,0:T(8,128)S(1)} fusion(f32[32,32,128]{2,1,0:T(8,128)S(1)} %pad_maximum_fusion.3, f32[32]{0:T(128)S(1)} %compare_convert_fusion.1, s32[32]{0:T(128)S(1)} %get-tuple-element.20), kind=kOutput, calls=%fused_computation.26 | convolution fusion | flops 50333696 | bytes 1048832 | tf_op jit(solution)/shard_map/kn,khr->hnr/dot_general | solution.py:25
  35.3 9.8 %collective-permute-done.1 = bf16[32,8192]{1,0:T(8,128)(2,1)S(1)} collective-permute-done((bf16[32,8192]{1,0:T(8,128)(2,1)S(1)}, bf16[32,8192]{1,0:T(8,128)(2,1)S(1)}, u32[]{:S(2)}, u32[]{:S(2)}) %collective-permute-start.1) | collective-permute-done | bytes 524320 | tf_op jit(solution)/shard_map/ppermute | solution.py:9
  45.8 2.4 %fusion.21 = f32[32,2,32,128]{3,2,1,0:T(8,128)S(1)} fusion(bf16[1,1,5,32,2,128,128]{6,5,4,3,2,1,0:T(8,128)(2,1)} %param.8, bf16[32,32,128]{2,1,0:T(8,128)(2,1)S(1)} %gather_fusion.2, pred[32]{0:T(512)(128)(4,1)S(1)} %get-tuple-element.21), kind=kOutput, calls=%fused_computation.22 | convolution fusion | flops 67239936 | bytes 3407904 | tf_op jit(solution)/shard_map/kprj,hkj->kphr/dot_general | solution.py:16
  48.3 1.1 %copy_bitcast_fusion.1 = bf16[32,64,128]{2,0,1:T(8,128)(2,1)S(1)} fusion(bf16[32,8192]{1,0:T(8,128)(2,1)} %collective-permute-done.3), kind=kLoop, calls=%fused_computation.36 | loop fusion | bytes 1048576 | tf_op jit(solution)/shard_map/reshape | solution.py:30
  50.1 2.4 %fusion.27 = f32[32,2,32,128]{3,2,1,0:T(8,128)S(1)} fusion(bf16[1,1,5,32,2,128,128]{6,5,4,3,2,1,0:T(8,128)(2,1)} %param.8, bf16[32,32,128]{2,1,0:T(8,128)(2,1)S(1)} %gather_fusion.4, pred[32]{0:T(512)(128)(4,1)S(1)} %get-tuple-element.6), kind=kOutput, calls=%fused_computation.24 | convolution fusion | flops 67239936 | bytes 3407904 | tf_op jit(solution)/shard_map/kprj,hkj->kphr/dot_general | solution.py:16
  52.7 0.9 %convolution_bitcast_fusion.2 = f32[32,32,128]{2,1,0:T(8,128)S(1)} fusion(f32[32,32,128]{2,1,0:T(8,128)S(1)} %pad_maximum_fusion.2, f32[32]{0:T(128)S(1)} %compare_convert_fusion.2, s32[32]{0:T(128)S(1)} %get-tuple-element.17), kind=kOutput, calls=%fused_computation.27 | convolution fusion | flops 50333696 | bytes 1048832 | tf_op jit(solution)/shard_map/kn,khr->hnr/dot_general | solution.py:25
  53.6 1.0 %fusion.33 = f32[32,32,128]{2,1,0:T(8,128)S(1)} fusion(f32[32,32,128]{2,1,0:T(8,128)S(1)} %convolution_bitcast_fusion.1, f32[32,32,128]{2,1,0:T(8,128)S(1)} %convolution_bitcast_fusion.2, f32[32,32,128]{2,1,0:T(8,128)S(1)} %convolution_bitcast_fusion.3, f32[32,32,128]{2,1,0:T(8,128)S(1)} %bitcast.237, f32[32,32,128]{2,1,0:T(8,128)S(1)} %pad_maximum_fusion, ...), kind=kOutput, calls=%fused_computation.33 | convolution fusion | flops 50857984 | bytes 3145984 | tf_op jit(solution)/shard_map/kn,khr->hnr/dot_general | solution.py:25
  54.6 0.9 %fusion.34 = f32[32,32,128]{2,1,0:T(8,128)S(1)} fusion(f32[32,32,128]{2,1,0:T(8,128)S(1)} %fusion.33, f32[32,32,128]{2,1,0:T(8,128)S(1)} %pad_maximum_fusion.4, f32[32]{0:T(128)S(1)} %compare_convert_fusion, s32[32]{0:T(128)S(1)} %get-tuple-element.16), kind=kOutput, calls=%fused_computation.34 | convolution fusion | flops 50464768 | bytes 1573120 | tf_op jit(solution)/shard_map/kn,khr->hnr/dot_general | solution.py:25
  55.5 1.1 %copy.94 = f32[4,8,32,128]{3,1,2,0:T(8,128)} copy(f32[4,8,32,128]{3,2,1,0:T(8,128)S(1)} %bitcast.238) | data formatting | bytes 1048576
  (36 shorter events, 5.9 us)
Async XLA Ops:
  9.0 14.2 %collective-permute-start = (bf16[32,8192]{1,0:T(8,128)(2,1)S(1)}, bf16[32,8192]{1,0:T(8,128)(2,1)S(1)}, u32[]{:S(2)}, u32[]{:S(2)}) collective-permute-start(bf16[32,8192]{1,0:T(8,128)(2,1)S(1)} %all_gather.3), channel_id=1, source_target_pairs={{0,2},{2,4},{4,6},{6,8},{8,10},{10,12},{12,14},{14,16},{16,18},{18... | collective-permute-start | bytes 1572872 | tf_op jit(solution)/shard_map/ppermute | solution.py:9
  11.5 15.0 %collective-permute-start.2 = (bf16[32,8192]{1,0:T(8,128)(2,1)S(1)}, bf16[32,8192]{1,0:T(8,128)(2,1)}, u32[]{:S(2)}, u32[]{:S(2)}) collective-permute-start(bf16[32,8192]{1,0:T(8,128)(2,1)S(1)} %all_gather.3), channel_id=1, source_target_pairs={{0,30},{2,0},{4,2},{6,4},{8,6},{10,8},{12,10},{14,12},{16,14},{18,... | collective-permute-start | bytes 1572872 | tf_op jit(solution)/shard_map/ppermute | solution.py:9
  30.8 14.3 %collective-permute-start.1 = (bf16[32,8192]{1,0:T(8,128)(2,1)S(1)}, bf16[32,8192]{1,0:T(8,128)(2,1)S(1)}, u32[]{:S(2)}, u32[]{:S(2)}) collective-permute-start(bf16[32,8192]{1,0:T(8,128)(2,1)S(1)} %collective-permute-done), channel_id=1, source_target_pairs={{0,2},{2,4},{4,6},{6,8},{8,10},{10,12},{12,14},{14,16},{16,18},{18... | collective-permute-start | bytes 1572872 | tf_op jit(solution)/shard_map/ppermute | solution.py:9
  33.4 14.9 %collective-permute-start.3 = (bf16[32,8192]{1,0:T(8,128)(2,1)}, bf16[32,8192]{1,0:T(8,128)(2,1)}, u32[]{:S(2)}, u32[]{:S(2)}) collective-permute-start(bf16[32,8192]{1,0:T(8,128)(2,1)} %collective-permute-done.2), channel_id=1, source_target_pairs={{0,30},{2,0},{4,2},{6,4},{8,6},{10,8},{12,10},{14,12},{16,14},{18,... | collective-permute-start | bytes 1572872 | tf_op jit(solution)/shard_map/ppermute | solution.py:9
where the time goes:
time: 57.1 us; the launch traced here: 56.6 us
  matrix products  16.8 us (29%)
  waiting for transfers between devices  11 us (19%)
  blocking collectives  9.02 us (16%)
  local copies, waits for them, and re-layouts  8.95 us (16%)
  other arithmetic  5.46 us (10%)
  starting transfers between devices  5.1 us (9%)
    dot_general x5, matrix products, block_terms(): jnp.einsum('kprj,hkj->kphr', slot_tiles, picked, preferred_element_type=j...  12.2 us
    ppermute x4, waiting for transfers between devices, passed_along(): lax.ppermute(array, axis, [(i, (i + by) % devices) for i in range(devices)])  11 us
    all_gather x1, blocking collectives, on_device(): group_x = lax.all_gather(strengths, 'row', axis=1, tiled=True)  9.02 us
    ppermute x4, starting transfers between devices, passed_along(): lax.ppermute(array, axis, [(i, (i + by) % devices) for i in range(devices)])  5.1 us
    dot_general x5, matrix products, block_terms(): jnp.einsum('kn,khr->hnr', onehot, combined, precision=lax.Precision.HIGHEST)  4.6 us
    convert_element_type x5, other arithmetic, block_terms(): (jnp.arange(capacity, dtype=jnp.int32) < live_count).astype(jnp.float32)  3.1 us
    gather x5, local copies, waits for them, and re-layouts, pick_blocks(): return jnp.take(blocks, slot_cols, axis=1)  3.01 us
    reshape x5, local copies, waits for them, and re-layouts, pick_blocks(): blocks = group_x.reshape(channels, -1, block_size)  2.54 us
  transfers between devices with their start and end apart: 4, of which 2 were waited for; matrix products, arithmetic and copies ran while one was open for 33% of the time, Pallas kernels for 0%

commit v1 on v0

--- a/solution.py
+++ b/solution.py
@@ -2,6 +2,18 @@
 import jax.numpy as jnp
 from jax import lax
 from jax.sharding import PartitionSpec as P
+
+
+def collect(value, axis, dim):
+    ways, here, lap = (lax.axis_size(axis), lax.axis_index(axis), value.shape[dim])
+    line, have = (value, 1)
+    while have < ways:
+        line = jnp.concatenate(
+            [line, lax.ppermute(line, axis, [(d, (d - have) % ways) for d in range(ways)])],
+            axis=dim,
+        )
+        have = 2 * have
+    return jnp.roll(line, here * lap, axis=dim)
 
 
 def passed_along(array, axis, by):
@@ -63,7 +75,7 @@
         picked = pick_blocks(group_x, source_block[0, 0, index], block_size)
         return apply_picked(totals_now, offset, picked)
 
-    group_x = lax.all_gather(strengths, "row", axis=1, tiled=True)
+    group_x = collect(strengths, "row", 1)
     for offset, source_x in window(group_x, reach):
         totals = apply_offset(totals, offset, source_x)
     return totals.reshape(channels, row_count)

time: 57.1 us -> 58.5 us (1.025)
  blocking collectives: 9.02 us -> 0 us
  waiting for transfers between devices: 11 us -> 17.7 us
  starting transfers between devices: 5.1 us -> 6.82 us
  other arithmetic: 5.46 us -> 7.06 us
    all_gather x1 -> x0, blocking collectives: 9.02 us -> none  [on_device(): group_x = lax.all_gather(strengths, 'row', axis=1, tiled=True)]
    ppermute x4, waiting for transfers between devices: 11 us -> 17.7 us  [passed_along(): lax.ppermute(array, axis, [(i, (i + by) % devices) for i in range(devices)])]
    ppermute x0 -> x1, starting transfers between devices: none -> 2.07 us  [collect(): lax.ppermute(line, axis, [(d, (d - have) % ways) for d in range(ways)])]
    concatenate x0 -> x1, other arithmetic: none -> 1.51 us  [collect(): return jnp.roll(line, here * lap, axis=dim)]
  transfers between devices with their start and end apart: 4 -> 5, of which waited for: 2 -> 2; matrix products, arithmetic and copies ran while one was open for 33% -> 33% of each run, Pallas kernels for 0% -> 0%
where the time goes in v1:
time: 58.5 us; the launch traced here: 57.7 us
  waiting for transfers between devices  17.7 us (30%)
  matrix products  16.8 us (29%)
  local copies, waits for them, and re-layouts  8.97 us (15%)
  other arithmetic  7.06 us (12%)
  starting transfers between devices  6.82 us (12%)
    ppermute x4, waiting for transfers between devices, passed_along(): lax.ppermute(array, axis, [(i, (i + by) % devices) for i in range(devices)])  17.7 us
    dot_general x5, matrix products, block_terms(): jnp.einsum('kprj,hkj->kphr', slot_tiles, picked, preferred_element_type=j...  12.2 us
    ppermute x4, starting transfers between devices, passed_along(): lax.ppermute(array, axis, [(i, (i + by) % devices) for i in range(devices)])  4.75 us
    dot_general x5, matrix products, block_terms(): jnp.einsum('kn,khr->hnr', onehot, combined, precision=lax.Precision.HIGHEST)  4.61 us
    convert_element_type x5, other arithmetic, block_terms(): (jnp.arange(capacity, dtype=jnp.int32) < live_count).astype(jnp.float32)  3.16 us
    gather x5, local copies, waits for them, and re-layouts, pick_blocks(): return jnp.take(blocks, slot_cols, axis=1)  3.01 us
    reshape x5, local copies, waits for them, and re-layouts, pick_blocks(): blocks = group_x.reshape(channels, -1, block_size)  2.54 us
    ppermute x1, starting transfers between devices, collect(): lax.ppermute(line, axis, [(d, (d - have) % ways) for d in range(ways)])  2.07 us
  transfers between devices with their start and end apart: 5, of which 2 were waited for; matrix products, arithmetic and copies ran while one was open for 33% of the time, Pallas kernels for 0%

profile of v1, /device:TPU:1, one launch (start us, length us, event | category | flops | bytes accessed | tf_op | source)
XLA Modules:
  0.0 57.7 jit_solution(1596278789225275395)
XLA Ops:
  0.0 2.1 %collective-permute-start = (bf16[32,4096]{1,0:T(8,128)(2,1)}, bf16[32,4096]{1,0:T(8,128)(2,1)S(1)}, u32[]{:S(2)}, u32[]{:S(2)}) collective-permute-start(bf16[32,4096]{1,0:T(8,128)(2,1)} %param.7), channel_id=1, source_target_pairs={{0,1},{1,0},{2,3},{3,2},{4,5},{5,4},{6,7},{7,6},{8,9},{9,8},{10,11... | collective-permute-start | bytes 786440 | tf_op jit(solution)/shard_map/ppermute | solution.py:12
  2.1 1.0 %multiply_bitcast_fusion = f32[4,8,32,128]{3,1,2,0:T(8,128)S(1)} fusion(bf16[32,4096]{1,0:T(8,128)(2,1)} %param.7), kind=kLoop, calls=%fused_computation.58 | loop fusion | flops 262144 | bytes 786432
  3.1 0.7 %compare_and_fusion = (pred[32]{0:T(512)(128)(4,1)S(1)}, s32[32]{0:T(128)S(1)}, pred[32]{0:T(512)(128)(4,1)S(1)}, s32[32]{0:T(128)S(1)}, pred[32]{0:T(512)(128)(...) fusion(s32[1,1,5,32]{3,1,2,0:T(1,128)} %param.10), kind=kLoop, calls=%fused_computation.149 | loop fusion | flops 960 | bytes 1440 | tf_op jit(solution)/shard_map/jit(_take)/and | solution.py:43
  3.8 1.5 %fusion.113 = (s32[1,1,1]{2,1,0:T(1,128)}, s32[1,1,1]{2,1,0:T(1,128)}, s32[1,1,1]{2,1,0:T(1,128)}, s32[1,1,1]{2,1,0:T(1,128)}, s32[1,1,1]{2,1,0:T(1,128)}) fusion(s32[1,1,5]{2,1,0:T(1,128)} %param.11), kind=kLoop, calls=%fused_computation.174 | loop fusion | bytes 40 | tf_op jit(solution)/shard_map/slice | solution.py:68
  5.9 0.7 %compare_convert_fusion.3 = f32[32]{0:T(128)S(1)} fusion(s32[]{:T(128)} %bitcast.21), kind=kLoop, calls=%fused_computation.157 | loop fusion | flops 64 | bytes 132 | tf_op jit(solution)/shard_map/convert_element_type | solution.py:32
  8.7 0.7 %slice_bitcast_fusion.10 = (s32[32]{0:T(128)S(1)}, s32[32]{0:T(128)S(1)}, s32[32]{0:T(128)S(1)}, s32[32]{0:T(128)S(1)}, s32[32]{0:T(128)S(1)}) fusion(s32[1,1,5,32]{3,1,2,0:T(1,128)} %param.9), kind=kLoop, calls=%fused_computation.159 | loop fusion | bytes 1280 | tf_op jit(solution)/shard_map/eq | solution.py:33
  9.5 1.5 %fusion.37 = bf16[32,8192]{1,0:T(8,128)(2,1)S(1)} fusion(s32[]{:T(128)S(6)} %select_n.21, bf16[32,4096]{1,0:T(8,128)(2,1)} %param.7, bf16[32,4096]{1,0:T(8,128)(2,1)S(1)} %collective-permute-done), kind=kLoop, calls=%fused_computation.41 | loop fusion | flops 2097152 | bytes 1048580 | tf_op jit(solution)/shard_map/jit(_roll_dynamic)/concatenate | solution.py:16
  11.0 2.1 %collective-permute-start.1 = (bf16[32,8192]{1,0:T(8,128)(2,1)S(1)}, bf16[32,8192]{1,0:T(8,128)(2,1)S(1)}, u32[]{:S(2)}, u32[]{:S(2)}) collective-permute-start(bf16[32,8192]{1,0:T(8,128)(2,1)S(1)} %fusion.37), channel_id=1, source_target_pairs={{0,2},{2,4},{4,6},{6,8},{8,10},{10,12},{12,14},{14,16},{16,18},{18... | collective-permute-start | bytes 1572872 | tf_op jit(solution)/shard_map/ppermute | solution.py:21
  13.8 2.4 %fusion.15 = f32[32,2,32,128]{3,2,1,0:T(8,128)S(1)} fusion(bf16[1,1,5,32,2,128,128]{6,5,4,3,2,1,0:T(8,128)(2,1)} %param.8, bf16[32,32,128]{2,1,0:T(8,128)(2,1)S(1)} %gather_fusion, pred[32]{0:T(512)(128)(4,1)S(1)} %get-tuple-element.25), kind=kOutput, calls=%fused_computation.20 | convolution fusion | flops 67239936 | bytes 3407904 | tf_op jit(solution)/shard_map/kprj,hkj->kphr/dot_general | solution.py:28
  16.4 8.4 %collective-permute-done.1 = bf16[32,8192]{1,0:T(8,128)(2,1)S(1)} collective-permute-done((bf16[32,8192]{1,0:T(8,128)(2,1)S(1)}, bf16[32,8192]{1,0:T(8,128)(2,1)S(1)}, u32[]{:S(2)}, u32[]{:S(2)}) %collective-permute-start.1) | collective-permute-done | bytes 524320 | tf_op jit(solution)/shard_map/ppermute | solution.py:21
  25.5 2.4 %fusion.18 = f32[32,2,32,128]{3,2,1,0:T(8,128)S(1)} fusion(bf16[1,1,5,32,2,128,128]{6,5,4,3,2,1,0:T(8,128)(2,1)} %param.8, bf16[32,32,128]{2,1,0:T(8,128)(2,1)S(1)} %gather_fusion.1, pred[32]{0:T(512)(128)(4,1)S(1)} %get-tuple-element.23), kind=kOutput, calls=%fused_computation.21 | convolution fusion | flops 67239936 | bytes 3407904 | tf_op jit(solution)/shard_map/kprj,hkj->kphr/dot_general | solution.py:28
  28.0 1.1 %copy_bitcast_fusion.2 = bf16[32,64,128]{2,0,1:T(8,128)(2,1)S(1)} fusion(bf16[32,8192]{1,0:T(8,128)(2,1)} %collective-permute-done.3), kind=kLoop, calls=%fused_computation.44 | loop fusion | bytes 1048576 | tf_op jit(solution)/shard_map/reshape | solution.py:42
  29.8 2.4 %fusion.24 = f32[32,2,32,128]{3,2,1,0:T(8,128)S(1)} fusion(bf16[1,1,5,32,2,128,128]{6,5,4,3,2,1,0:T(8,128)(2,1)} %param.8, bf16[32,32,128]{2,1,0:T(8,128)(2,1)S(1)} %gather_fusion.3, pred[32]{0:T(512)(128)(4,1)S(1)} %get-tuple-element.27), kind=kOutput, calls=%fused_computation.23 | convolution fusion | flops 67239936 | bytes 3407904 | tf_op jit(solution)/shard_map/kprj,hkj->kphr/dot_general | solution.py:28
  32.4 2.5 %collective-permute-start.2 = (bf16[32,8192]{1,0:T(8,128)(2,1)S(1)}, bf16[32,8192]{1,0:T(8,128)(2,1)S(1)}, u32[]{:S(2)}, u32[]{:S(2)}) collective-permute-start(bf16[32,8192]{1,0:T(8,128)(2,1)S(1)} %collective-permute-done.1), channel_id=1, source_target_pairs={{0,2},{2,4},{4,6},{6,8},{8,10},{10,12},{12,14},{14,16},{16,18},{18... | collective-permute-start | bytes 1572872 | tf_op jit(solution)/shard_map/ppermute | solution.py:21
  35.0 0.9 %convolution_bitcast_fusion.3 = f32[32,32,128]{2,1,0:T(8,128)S(1)} fusion(f32[32,32,128]{2,1,0:T(8,128)S(1)} %pad_maximum_fusion.1, f32[32]{0:T(128)S(1)} %compare_convert_fusion.3, s32[32]{0:T(128)S(1)} %get-tuple-element.18), kind=kOutput, calls=%fused_computation.28 | convolution fusion | flops 50333696 | bytes 1048832 | tf_op jit(solution)/shard_map/kn,khr->hnr/dot_general | solution.py:37
  35.9 0.9 %convolution_bitcast_fusion.1 = f32[32,32,128]{2,1,0:T(8,128)S(1)} fusion(f32[32,32,128]{2,1,0:T(8,128)S(1)} %pad_maximum_fusion.3, f32[32]{0:T(128)S(1)} %compare_convert_fusion.1, s32[32]{0:T(128)S(1)} %get-tuple-element.20), kind=kOutput, calls=%fused_computation.26 | convolution fusion | flops 50333696 | bytes 1048832 | tf_op jit(solution)/shard_map/kn,khr->hnr/dot_general | solution.py:37
  36.9 9.3 %collective-permute-done.2 = bf16[32,8192]{1,0:T(8,128)(2,1)S(1)} collective-permute-done((bf16[32,8192]{1,0:T(8,128)(2,1)S(1)}, bf16[32,8192]{1,0:T(8,128)(2,1)S(1)}, u32[]{:S(2)}, u32[]{:S(2)}) %collective-permute-start.2) | collective-permute-done | bytes 524320 | tf_op jit(solution)/shard_map/ppermute | solution.py:21
  46.9 2.4 %fusion.21 = f32[32,2,32,128]{3,2,1,0:T(8,128)S(1)} fusion(bf16[1,1,5,32,2,128,128]{6,5,4,3,2,1,0:T(8,128)(2,1)} %param.8, bf16[32,32,128]{2,1,0:T(8,128)(2,1)S(1)} %gather_fusion.2, pred[32]{0:T(512)(128)(4,1)S(1)} %get-tuple-element.21), kind=kOutput, calls=%fused_computation.22 | convolution fusion | flops 67239936 | bytes 3407904 | tf_op jit(solution)/shard_map/kprj,hkj->kphr/dot_general | solution.py:28
  49.4 1.1 %copy_bitcast_fusion.1 = bf16[32,64,128]{2,0,1:T(8,128)(2,1)S(1)} fusion(bf16[32,8192]{1,0:T(8,128)(2,1)} %collective-permute-done.4), kind=kLoop, calls=%fused_computation.43 | loop fusion | bytes 1048576 | tf_op jit(solution)/shard_map/reshape | solution.py:42
  51.2 2.4 %fusion.27 = f32[32,2,32,128]{3,2,1,0:T(8,128)S(1)} fusion(bf16[1,1,5,32,2,128,128]{6,5,4,3,2,1,0:T(8,128)(2,1)} %param.8, bf16[32,32,128]{2,1,0:T(8,128)(2,1)S(1)} %gather_fusion.4, pred[32]{0:T(512)(128)(4,1)S(1)} %get-tuple-element.6), kind=kOutput, calls=%fused_computation.24 | convolution fusion | flops 67239936 | bytes 3407904 | tf_op jit(solution)/shard_map/kprj,hkj->kphr/dot_general | solution.py:28
  53.8 0.9 %convolution_bitcast_fusion.2 = f32[32,32,128]{2,1,0:T(8,128)S(1)} fusion(f32[32,32,128]{2,1,0:T(8,128)S(1)} %pad_maximum_fusion.2, f32[32]{0:T(128)S(1)} %compare_convert_fusion.2, s32[32]{0:T(128)S(1)} %get-tuple-element.17), kind=kOutput, calls=%fused_computation.27 | convolution fusion | flops 50333696 | bytes 1048832 | tf_op jit(solution)/shard_map/kn,khr->hnr/dot_general | solution.py:37
  54.7 1.0 %fusion.33 = f32[32,32,128]{2,1,0:T(8,128)S(1)} fusion(f32[32,32,128]{2,1,0:T(8,128)S(1)} %convolution_bitcast_fusion.1, f32[32,32,128]{2,1,0:T(8,128)S(1)} %convolution_bitcast_fusion.2, f32[32,32,128]{2,1,0:T(8,128)S(1)} %convolution_bitcast_fusion.3, f32[32,32,128]{2,1,0:T(8,128)S(1)} %bitcast.237, f32[32,32,128]{2,1,0:T(8,128)S(1)} %pad_maximum_fusion, ...), kind=kOutput, calls=%fused_computation.33 | convolution fusion | flops 50857984 | bytes 3145984 | tf_op jit(solution)/shard_map/kn,khr->hnr/dot_general | solution.py:37
  55.7 0.9 %fusion.34 = f32[32,32,128]{2,1,0:T(8,128)S(1)} fusion(f32[32,32,128]{2,1,0:T(8,128)S(1)} %fusion.33, f32[32,32,128]{2,1,0:T(8,128)S(1)} %pad_maximum_fusion.4, f32[32]{0:T(128)S(1)} %compare_convert_fusion, s32[32]{0:T(128)S(1)} %get-tuple-element.16), kind=kOutput, calls=%fused_computation.34 | convolution fusion | flops 50464768 | bytes 1573120 | tf_op jit(solution)/shard_map/kn,khr->hnr/dot_general | solution.py:37
  56.6 1.1 %copy.94 = f32[4,8,32,128]{3,1,2,0:T(8,128)} copy(f32[4,8,32,128]{3,2,1,0:T(8,128)S(1)} %bitcast.238) | data formatting | bytes 1048576
  (38 shorter events, 6.6 us)
Async XLA Ops:
  0.0 9.4 %collective-permute-start = (bf16[32,4096]{1,0:T(8,128)(2,1)}, bf16[32,4096]{1,0:T(8,128)(2,1)S(1)}, u32[]{:S(2)}, u32[]{:S(2)}) collective-permute-start(bf16[32,4096]{1,0:T(8,128)(2,1)} %param.7), channel_id=1, source_target_pairs={{0,1},{1,0},{2,3},{3,2},{4,5},{5,4},{6,7},{7,6},{8,9},{9,8},{10,11... | collective-permute-start | bytes 786440 | tf_op jit(solution)/shard_map/ppermute | solution.py:12
  11.0 13.8 %collective-permute-start.1 = (bf16[32,8192]{1,0:T(8,128)(2,1)S(1)}, bf16[32,8192]{1,0:T(8,128)(2,1)S(1)}, u32[]{:S(2)}, u32[]{:S(2)}) collective-permute-start(bf16[32,8192]{1,0:T(8,128)(2,1)S(1)} %fusion.37), channel_id=1, source_target_pairs={{0,2},{2,4},{4,6},{6,8},{8,10},{10,12},{12,14},{14,16},{16,18},{18... | collective-permute-start | bytes 1572872 | tf_op jit(solution)/shard_map/ppermute | solution.py:21
  13.2 14.9 %collective-permute-start.3 = (bf16[32,8192]{1,0:T(8,128)(2,1)S(1)}, bf16[32,8192]{1,0:T(8,128)(2,1)}, u32[]{:S(2)}, u32[]{:S(2)}) collective-permute-start(bf16[32,8192]{1,0:T(8,128)(2,1)S(1)} %fusion.37), channel_id=1, source_target_pairs={{0,30},{2,0},{4,2},{6,4},{8,6},{10,8},{12,10},{14,12},{16,14},{18,... | collective-permute-start | bytes 1572872 | tf_op jit(solution)/shard_map/ppermute | solution.py:21
  32.4 13.8 %collective-permute-start.2 = (bf16[32,8192]{1,0:T(8,128)(2,1)S(1)}, bf16[32,8192]{1,0:T(8,128)(2,1)S(1)}, u32[]{:S(2)}, u32[]{:S(2)}) collective-permute-start(bf16[32,8192]{1,0:T(8,128)(2,1)S(1)} %collective-permute-done.1), channel_id=1, source_target_pairs={{0,2},{2,4},{4,6},{6,8},{8,10},{10,12},{12,14},{14,16},{16,18},{18... | collective-permute-start | bytes 1572872 | tf_op jit(solution)/shard_map/ppermute | solution.py:21
  35.0 14.5 %collective-permute-start.4 = (bf16[32,8192]{1,0:T(8,128)(2,1)}, bf16[32,8192]{1,0:T(8,128)(2,1)}, u32[]{:S(2)}, u32[]{:S(2)}) collective-permute-start(bf16[32,8192]{1,0:T(8,128)(2,1)} %collective-permute-done.3), channel_id=1, source_target_pairs={{0,30},{2,0},{4,2},{6,4},{8,6},{10,8},{12,10},{14,12},{16,14},{18,... | collective-permute-start | bytes 1572872 | tf_op jit(solution)/shard_map/ppermute | solution.py:21
